TPU v7x, 512 devices: a whole 4x8x8 slice. The times are simulated.
512 devices in a mesh: frame: 16 (over x, y_lo, core), crop: 4 (over y_hi), dp: 8 (over z).
Axes of the slice: x: 4, y: 8 (y_hi: 4, y_lo: 2; y = y_hi * 2 + y_lo), z: 8, core: 2. Of those that a mesh axis runs over, the one named last changes fastest.
Arguments:
- global_clips: bfloat16 [8, 16, 256, 1408], P('dp', 'frame', 'crop'), may hold values from -6 to 6
- frame_map: int32 [8, 16, 8], P('dp', 'crop'), may hold values from 0 to 15
- teacher_qkv: bfloat16 [1408, 4224], P(None, 'frame'), may hold values from -0.15625 to 0.15625
- teacher_out: bfloat16 [1408, 1408], P('frame'), may hold values from -0.15625 to 0.15625
- teacher_bottle: bfloat16 [1408, 256], replicated, may hold values from -0.15625 to 0.15625
- student_qkv: bfloat16 [1408, 4224], P(None, 'frame'), may hold values from -0.15625 to 0.15625
- student_out: bfloat16 [1408, 1408], P('frame'), may hold values from -0.15625 to 0.15625
- student_bottle: bfloat16 [1408, 256], replicated, may hold values from -0.15625 to 0.15625
- prototypes: bfloat16 [256, 32768], P(None, 'frame'), may hold values from -1.796875 to 1.796875
- center: float32 [32768], P('frame'), may hold values from -8.6 to -3.9
Outputs:
- grad_qkv: float32 [1408, 4224], P(('crop', 'dp'), 'frame')
- grad_out: float32 [1408, 1408], P('frame', ('crop', 'dp'))
- grad_bottle: float32 [1408, 256], P(('crop', 'dp'))
All inputs are finite; a program needn't handle non-finite values.
Results may differ from a plain program's by a relative error of at most 0.00035.
Values may be sent and summed in bfloat16 or wider, within the bound.
No kernel may reach another device: no remote copies, remote signals or barrier semaphores. Data moves between devices by JAX's collectives and lax.ppermute only.
A program may use at most 64 MiB of HBM per device.

v0:
```python
import math
import jax
import jax.numpy as jnp
from jax import lax
from jax.sharding import PartitionSpec as P

D = 1408
HEADS = 16
HIGH = lax.Precision.HIGHEST
TAU_TEACH = 0.04
TAU_STUD = 0.1


def combined_all(value, axis, join):
    pieces = jax.tree.map(lambda part: lax.all_gather(part, axis), value)
    head = jax.tree.map(lambda part: part[0], pieces)
    tail = jax.tree.map(lambda part: part[1:], pieces)
    running, _ = lax.scan(lambda running, share: (join(running, share), None), head, tail)
    return running


def norm_tokens(tokens):
    values = tokens.astype(jnp.float32)
    middle = jnp.mean(values, axis=-1, keepdims=True)
    spread = jnp.mean(jnp.square(values - middle), axis=-1, keepdims=True)
    return ((values - middle) * lax.rsqrt(spread + 1e-06)).astype(jnp.bfloat16)


def attend_core(qkv):
    rounded = lax.optimization_barrier(qkv.astype(jnp.bfloat16)).astype(jnp.float32)
    query = rounded[:, :, :, 0]
    keys = rounded[:, :, :, 1]
    values = rounded[:, :, :, 2]
    scale = 1.0 / math.sqrt(qkv.shape[-1])
    scores = jnp.einsum("iphe,jphe->phij", query, keys, precision=HIGH) * scale
    weights = jax.nn.softmax(scores, axis=-1)
    weights = lax.optimization_barrier(weights.astype(jnp.bfloat16)).astype(jnp.float32)
    return jnp.einsum("phij,jphe->iphe", weights, values, precision=HIGH)


def project(normed, weight, heads_here):
    qkv = jnp.einsum("fpd,dc->fpc", normed, weight, preferred_element_type=jnp.float32)
    return qkv.reshape(normed.shape[0], normed.shape[1], heads_here, 3, -1)


def unit(vector):
    return vector * lax.rsqrt(jnp.sum(vector * vector, axis=-1, keepdims=True) + 1e-06)


def merge_pair(top_a, sum_a, vec_a, top_b, sum_b, vec_b):
    top = jnp.maximum(top_a, top_b)
    factor_a = jnp.exp(top_a - top)
    factor_b = jnp.exp(top_b - top)
    return (
        top,
        sum_a * factor_a + sum_b * factor_b,
        vec_a * factor_a[..., None] + vec_b * factor_b[..., None],
    )


def combine_totals(first, second):
    student = merge_pair(first[0], first[1], first[2], second[0], second[1], second[2])
    teacher = merge_pair(first[3], first[4], first[5], second[3], second[4], second[5])
    return (student[0], student[1], student[2], teacher[0], teacher[1], teacher[2])


def local(
    global_clips,
    frame_map,
    teacher_qkv,
    teacher_out,
    teacher_bottle,
    student_qkv,
    student_out,
    student_bottle,
    prototypes,
    center,
):
    head_size = D // HEADS
    heads_here = teacher_out.shape[0] // head_size
    tokens = global_clips[0]
    gathered = lax.all_gather(tokens, "frame", axis=0, tiled=True)
    frames_all, patches_here = (gathered.shape[0], gathered.shape[1])
    normed = norm_tokens(gathered)
    teacher_count = frames_all * patches_here * lax.axis_size("crop")
    t_att = attend_core(project(normed, teacher_qkv, heads_here))
    t_heads = jnp.sum(t_att, axis=(0, 1)).reshape(-1)
    t_out32 = teacher_out.astype(jnp.float32)
    t_partial = (
        jnp.sum(tokens, axis=(0, 1), dtype=jnp.float32) + jnp.dot(t_heads, t_out32, precision=HIGH)
    ) / teacher_count
    maps = frame_map[0]
    clips_here, local_frames = maps.shape
    order = maps.T.reshape(-1)
    frame_qkv = jnp.einsum(
        "fpd,dc->fpc", normed, student_qkv, preferred_element_type=jnp.float32
    ).astype(jnp.bfloat16)
    picked = jnp.take(frame_qkv, order, axis=0)
    s_qkv = picked.reshape(local_frames, clips_here * patches_here, heads_here, 3, -1)
    s_att = attend_core(s_qkv)
    local_count = local_frames * patches_here
    s_heads = (
        jnp.sum(s_att.reshape(local_frames, clips_here, patches_here, -1), axis=(0, 2))
        / local_count
    )
    s_out32 = student_out.astype(jnp.float32)
    s_partial = jnp.dot(s_heads, s_out32, precision=HIGH)
    frame_sums = jnp.sum(gathered, axis=1, dtype=jnp.float32)
    picks = jnp.sum(
        (maps[:, :, None] == jnp.arange(frames_all, dtype=jnp.int32)[None, None, :]).astype(
            jnp.float32
        ),
        axis=1,
    )
    local_mean = jnp.dot(picks, frame_sums, precision=HIGH) / local_count
    t_pooled = lax.psum(t_partial, ("frame", "crop"))
    s_summed = lax.psum(s_partial, "frame")
    s_pooled = local_mean + s_summed
    protos = prototypes.astype(jnp.float32)
    s_bottle32 = student_bottle.astype(jnp.float32)
    unit_t = unit(jnp.dot(t_pooled, teacher_bottle.astype(jnp.float32), precision=HIGH))
    s_z = jnp.dot(s_pooled, s_bottle32, precision=HIGH)
    unit_s = unit(s_z)
    t_logits = (jnp.dot(unit_t, protos, precision=HIGH) - center) / TAU_TEACH
    s_logits = jnp.dot(unit_s, protos, precision=HIGH) / TAU_STUD
    t_top = jnp.max(t_logits)
    t_exp = jnp.exp(t_logits - t_top)
    s_top = jnp.max(s_logits, axis=-1)
    s_exp = jnp.exp(s_logits - s_top[:, None])
    merged = combined_all(
        (
            s_top,
            jnp.sum(s_exp, axis=-1),
            jnp.dot(s_exp, protos.T, precision=HIGH),
            t_top,
            jnp.sum(t_exp),
            jnp.dot(protos, t_exp, precision=HIGH),
        ),
        "frame",
        combine_totals,
    )
    s_expect = merged[2] / merged[1][:, None]
    t_expect = merged[5] / merged[4]
    all_clips = clips_here * lax.axis_size("crop")
    d_unit = (s_expect - t_expect[None, :]) / (all_clips * TAU_STUD)
    inverse = lax.rsqrt(jnp.sum(s_z * s_z, axis=-1, keepdims=True) + 1e-06)
    d_z = (d_unit - unit_s * jnp.sum(unit_s * d_unit, axis=-1, keepdims=True)) * inverse
    g_bottle = jnp.dot(s_pooled.T, d_z, precision=HIGH)
    d_pooled = jnp.dot(d_z, s_bottle32.T, precision=HIGH)
    g_out = jnp.dot(s_heads.T, d_pooled, precision=HIGH)
    d_heads = jnp.dot(d_pooled, s_out32.T, precision=HIGH) / local_count
    d_att = jnp.broadcast_to(
        d_heads[None, :, None, :], (local_frames, clips_here, patches_here, d_heads.shape[1])
    ).reshape(s_att.shape)
    _, core_back = jax.vjp(attend_core, s_qkv)
    d_qkv = core_back(d_att)[0].reshape(local_frames * clips_here, patches_here, -1)
    selector = (order[:, None] == jnp.arange(frames_all, dtype=jnp.int32)[None, :]).astype(
        jnp.bfloat16
    )
    d_frames = jnp.einsum("rf,rpc->fpc", selector, d_qkv, preferred_element_type=jnp.float32)
    g_qkv = jnp.einsum("fpd,fpc->dc", normed.astype(jnp.float32), d_frames, precision=HIGH)
    summed = (
        lax.psum_scatter(g_qkv, ("crop", "dp"), scatter_dimension=0, tiled=True),
        lax.psum_scatter(g_out, ("crop", "dp"), scatter_dimension=1, tiled=True),
        lax.psum_scatter(g_bottle, ("crop", "dp"), scatter_dimension=0, tiled=True),
    )
    return (summed[0], summed[1], summed[2])


def solution(mesh):
    return jax.shard_map(
        local,
        mesh=mesh,
        in_specs=(
            P("dp", "frame", "crop", None),
            P("dp", "crop", None),
            P(None, "frame"),
            P("frame", None),
            P(),
            P(None, "frame"),
            P("frame", None),
            P(),
            P(None, "frame"),
            P("frame"),
        ),
        out_specs=(P(("crop", "dp"), "frame"), P("frame", ("crop", "dp")), P(("crop", "dp"), None)),
        check_vma=False,
    )
```

profile of v0, /device:TPU:26, one launch (start us, length us, event | category | flops | bytes accessed | tf_op | source)
XLA Modules:
  0.0 642.9 jit_solution(15766449092448168126)
XLA Ops:
  7.2 0.7 all-gather.9.cloned.1.call-update
  7.9 0.8 copy.44
  8.8 0.7 eq.28
  9.4 1.3 dynamic-slice
  11.4 0.8 convert_reduce_fusion.3
  12.2 1.6 convert_reduce_fusion.2
  13.7 0.7 compare_and_fusion
  14.4 39.3 %all-gather.9.cloned.1.call-done = bf16[16,1,64,1408]{3,2,1,0:T(8,128)(2,1)} async-done(((bf16[1,1,64,1408]{3,2,1,0:T(8,128)(2,1)}), bf16[16,1,64,1408]{3,2,1,0:T(8,128)(2,1)}) %all-gather.9.cloned.1.call-update) | async-done | bytes 2883600 | tf_op jit(solution)/shard_map/all_gather | solution.py:82
  53.7 3.4 convert_reduce_fusion
  57.1 0.9 fusion.16
  58.6 1.9 fusion.26
  60.5 1.9 gather_fusion
  62.4 4.5 reshape.311
  67.0 1.3 copy_select_fusion
  68.8 6.9 %fusion.83 = (f32[256,8]{1,0:T(8,128)S(1)}, f32[256,8,8]{1,2,0:T(8,128)S(1)}) fusion(f32[256,8,8]{1,2,0:T(8,128)S(1)} %convolution_multiply_fusion.2), kind=kOutput, calls=%fused_computation.133 | output fusion | flops 32775 | bytes 139264 | tf_op jit(solution)/shard_map/sub | solution.py:36
  76.9 45.0 %psum.14 = f32[4,1408]{1,0:T(4,128)S(1)} all-reduce(f32[4,1408]{1,0:T(4,128)S(1)} %fusion.67), channel_id=1, replica_groups=mesh['frame'=16,'crop'=4,'dp'=8] {'frame'}, use_global_device_ids=true, to_apply=%region_8.9 | all-reduce | flops 5632 | bytes 45056 | tf_op jit(solution)/shard_map/psum | solution.py:117
  122.6 0.7 fusion.84
  123.3 0.8 fusion.56
  124.1 0.9 convolution_bitcast_fusion.5
  125.0 25.2 %all-gather.5 = f32[16,4,256]{2,1,0:T(4,128)S(1)} all-gather(f32[1,4,256]{2,1,0:T(4,128)S(1)} %convolution_bitcast_fusion.5), channel_id=5, replica_groups=mesh['frame'=16,'crop'=4,'dp'=8] {'frame'}, dimensions={0}, use_global_device_ids=true | all-gather | bytes 69632 | tf_op jit(solution)/shard_map/all_gather | solution.py:15
  150.9 3.9 fusion.29
  154.8 2.7 convert_element_type.84
  157.5 2.0 fusion.82
  159.5 1.4 convolution_multiply_fusion.3
  161.0 2.1 fusion.38
  163.1 1.4 fusion.39
  164.5 1.2 convolution_reduce_fusion.1
  165.7 123.4 %psum.15 = f32[1408]{0:T(1024)S(1)} all-reduce(f32[1408]{0:T(1024)S(1)} %add_multiply_fusion), channel_id=1, replica_groups=mesh['frame'=16,'crop'=4,'dp'=8] {'frame','crop'}, use_global_device_ids=true, to_apply=%region_16.17 | all-reduce | flops 1408 | bytes 11264 | tf_op jit(solution)/shard_map/psum | solution.py:116
  292.0 1.3 fusion.81
  293.3 0.9 convolution_bitcast_fusion.6
  294.2 20.8 %all-gather.6 = f32[16,1,256]{2,1,0:T(1,128)S(1)} all-gather(f32[1,1,256]{2,1,0:T(1,128)S(1)} %convolution_bitcast_fusion.6), channel_id=6, replica_groups=mesh['frame'=16,'crop'=4,'dp'=8] {'frame'}, dimensions={0}, use_global_device_ids=true | all-gather | bytes 17408 | tf_op jit(solution)/shard_map/all_gather | solution.py:15
  315.6 1.4 dynamic-update-slice.2
  316.9 1.4 dynamic-update-slice.3
  318.3 24.0 %all-reduce.13 = (f32[64]{0:T(128)S(1)}, f32[64]{0:T(128)S(1)}, f32[16]{0:T(128)}, f32[16]{0:T(128)}) all-reduce(f32[64]{0:T(128)S(1)} %dynamic-update-slice, f32[64]{0:T(128)S(1)} %dynamic-update-slice.1, f32[16]{0:T(128)S(1)} %dynamic-update-slice.2, f32[16]{0:T(128)S(1)} %dynamic-update-slice.3), channel_id=3, replica_groups=mesh['frame'=16,'crop'=4,'dp'=8] {'frame'}, use_global_device_ids=true, to_apply=%add.3 | all-reduce | flops 160 | bytes 1280
  342.6 0.7 slice.72
  343.4 0.7 slice.73
  344.1 86.0 %while.20 = (s32[]{:T(128)}, f32[4]{0:T(128)S(1)}, f32[4]{0:T(128)S(1)}, f32[4,256]{1,0:T(4,128)S(1)}, f32[]{:T(128)}, /*index=5*/f32[]{:T(128)}, f32[256]{0:T(2...) while((s32[]{:T(128)}, f32[4]{0:T(128)S(1)}, ...), condition=%wide.region_21.22_spmd, body=%wide.region_20.21_spmd.sunk | while | flops 3872 | bytes 17849 | solution.py:18
  352.5 0.6 dynamic_slice.51
  430.9 0.7 fusion.76
  432.0 2.0 fusion.36
  434.5 1.3 convolution_bitcast_fusion.1
  435.8 1.2 convolution_bitcast_fusion.2
  437.0 1.0 convolution_bitcast_fusion.3
  438.0 2.2 fusion.65
  440.1 2.5 fusion.75
  442.9 2.0 copy.54
  444.9 2.8 reshape.240
  447.8 5.8 copy.55
  453.6 1.9 fusion.59
  455.9 6.9 %convolution_bitcast_fusion = f32[1408,264]{1,0:T(8,128)} fusion(f32[16,64,264]{2,0,1:T(8,128)S(1)} %fusion.59, bf16[16,1,64,1408]{3,2,1,0:T(8,128)(2,1)S(1)} %copy-done.3, f32[16,64]{1,0:T(8,128)S(1)} %copy-done.27, f32[16,64]{1,0:T(8,128)S(1)} %copy-done.20), kind=kOutput, calls=%fused_computation.27 | convolution fusion | flops 4573364224 | bytes 5459968 | tf_op jit(solution)/shard_map/fpd,fpc->dc/dot_general | solution.py:161
  462.8 125.1 %fusion.79 = (f32[48,264]{1,0:T(8,128)S(1)}, f32[88,48]{0,1:T(8,128)S(1)}, f32[48,256]{1,0:T(8,128)S(1)}) fusion(f32[1408,264]{1,0:T(8,128)} %convolution_bitcast_fusion, f32[88,1408]{0,1:T(8,128)S(1)} %copy-done.7, f32[1408,256]{1,0:T(8,128)S(1)} %copy-done.6), kind=kCustom, calls=%all-reduce-scatter.3 | all-reduce-scatter fusion | flops 933889 | bytes 3543040
  587.8 1.9 collective-permute-start.4
  589.8 1.9 collective-permute-start.3
  591.7 1.9 collective-permute-start.5
  593.6 1.3 dynamic-slice.12
  595.6 11.1 %collective-permute-start.1 = (f32[48,264]{1,0:T(8,128)S(1)}, f32[48,264]{1,0:T(8,128)S(1)}, u32[]{:S(2)}, u32[]{:S(2)}) collective-permute-start(f32[48,264]{1,0:T(8,128)S(1)} %get-tuple-element.112), channel_id=1, source_target_pairs={{0,2},{1,3},{2,4},{3,5},{4,6},{5,7},{6,8},{7,9},{8,10},{9,11},{10,... | collective-permute-start | bytes 152072
  606.6 1.9 collective-permute-start
  608.6 2.5 collective-permute-start.7
  611.1 1.9 collective-permute-start.6
  613.0 2.3 collective-permute-start.8
  616.5 7.7 %collective-permute-done.8 = f32[28,256]{1,0:T(8,128)S(1)} collective-permute-done((f32[28,256]{1,0:T(8,128)S(1)}, f32[28,256]{1,0:T(8,128)S(1)}, u32[]{:S(2)}, u32[]{:S(2)}) %collective-permute-start.8) | collective-permute-done | bytes 28704
  624.1 1.9 collective-permute-start.2
  627.2 7.7 %collective-permute-done.2 = f32[28,264]{1,0:T(8,128)S(1)} collective-permute-done((f32[28,264]{1,0:T(8,128)S(1)}, f32[28,264]{1,0:T(8,128)S(1)}, u32[]{:S(2)}, u32[]{:S(2)}) %collective-permute-start.2) | collective-permute-done | bytes 29600
  635.4 0.6 constant_dynamic-slice_fusion.5
  (222 shorter events, 31.4 us)
Async XLA Ops:
  7.2 115.4 %copy-start = (bf16[256,2048]{1,0:T(8,128)(2,1)S(1)}, bf16[256,2048]{1,0:T(8,128)(2,1)}, u32[]{:S(2)}) copy-start(bf16[256,2048]{1,0:T(8,128)(2,1)} %param.20) | copy-start | bytes 3145732
  7.2 46.5 %all-gather.9.cloned.1.call-start = ((), (), s32[]{:S(2)}) async-start(), calls=%async_computation | async-start | bytes 3063808 | tf_op jit(solution)/shard_map/all_gather | solution.py:82
  53.7 3.4 copy-start.1
  57.1 1.5 copy-start.35
  57.1 0.9 copy-start.18
  58.0 0.6 copy-start.25
  68.3 7.5 %copy-start.4 = (bf16[8,256,1,3,88]{4,0,1,3,2:T(8,128)(2,1)}, bf16[8,256,1,3,88]{4,0,1,3,2:T(8,128)(2,1)S(1)}, u32[]{:S(2)}) copy-start(bf16[8,256,1,3,88]{4,0,1,3,2:T(8,128)(2,1)S(1)} %copy_select_fusion) | copy-start | bytes 3244036
  68.8 7.9 %copy-start.10 = (bf16[88,1408]{1,0:T(8,128)(2,1)S(1)}, bf16[88,1408]{1,0:T(8,128)(2,1)}, u32[]{:S(2)}) copy-start(bf16[88,1408]{1,0:T(8,128)(2,1)} %param.18) | copy-start | bytes 743428
  75.6 46.2 %copy-start.14 = (f32[16,1408]{1,0:T(8,128)S(1)}, f32[16,1408]{1,0:T(8,128)}, u32[]{:S(2)}) copy-start(f32[16,1408]{1,0:T(8,128)} %get-tuple-element.77) | copy-start | bytes 270340
  75.7 46.4 %copy-start.12 = (bf16[1408,256]{1,0:T(8,128)(2,1)S(1)}, bf16[1408,256]{1,0:T(8,128)(2,1)}, u32[]{:S(2)}) copy-start(bf16[1408,256]{1,0:T(8,128)(2,1)} %param.19) | copy-start | bytes 2162692
  75.8 0.8 copy-start.8
  76.6 74.2 %copy-start.19 = (f32[16,64]{1,0:T(8,128)S(1)}, f32[16,64]{1,0:T(8,128)}, u32[]{:S(2)}) copy-start(f32[16,64]{1,0:T(8,128)} %copy-done.18) | copy-start | bytes 12292
  76.6 74.2 %copy-start.26 = (f32[16,64]{1,0:T(8,128)S(1)}, f32[16,64]{1,0:T(8,128)}, u32[]{:S(2)}) copy-start(f32[16,64]{1,0:T(8,128)} %copy-done.25) | copy-start | bytes 12292
  76.7 73.6 %copy-start.23 = (f32[4,88]{1,0:T(4,128)}, f32[4,88]{1,0:T(4,128)S(1)}, u32[]{:S(2)}) copy-start(f32[4,88]{1,0:T(4,128)S(1)} %bitcast_reduce_fusion) | copy-start | bytes 4228
  121.9 29.0 %copy-start.2 = (bf16[16,1,64,1408]{3,2,1,0:T(8,128)(2,1)S(1)}, bf16[16,1,64,1408]{3,2,1,0:T(8,128)(2,1)}, u32[]{:S(2)}) copy-start(bf16[16,1,64,1408]{3,2,1,0:T(8,128)(2,1)} %all-gather.9.cloned.1.call-done) | copy-start | bytes 8650756
  122.6 2.4 copy-start.16
  122.6 0.7 copy-start.30
  123.3 27.0 %copy-start.28 = (f32[4]{0:T(128)}, f32[4]{0:T(128)S(1)}, u32[]{:S(2)}) copy-start(f32[4]{0:T(128)S(1)} %get-tuple-element.128) | copy-start | bytes 52
  150.2 0.6 copy-start.15
  159.5 6.2 copy-start.21
  159.5 129.6 %copy-start.11 = (bf16[1408,256]{1,0:T(8,128)(2,1)S(1)}, bf16[1408,256]{1,0:T(8,128)(2,1)}, u32[]{:S(2)}) copy-start(bf16[1408,256]{1,0:T(8,128)(2,1)} %param.16) | copy-start | bytes 2162692
  161.0 130.4 %copy-start.22 = (f32[2048]{0:T(1024)S(1)}, f32[2048]{0:T(1024)}, u32[]{:S(2)}) copy-start(f32[2048]{0:T(1024)} %param.21) | copy-start | bytes 24580
  163.1 152.0 %copy-start.29 = (f32[4]{0:T(128)S(1)}, f32[4]{0:T(128)}, u32[]{:S(2)}) copy-start(f32[4]{0:T(128)} %copy-done.28) | copy-start | bytes 52
  163.1 152.2 %copy-start.34 = (f32[4]{0:T(128)S(1)}, f32[4]{0:T(128)}, u32[]{:S(2)}) copy-start(f32[4]{0:T(128)} %fusion.56) | copy-start | bytes 52
  163.1 181.0 %slice-start = ((f32[16,4,256]{2,1,0:T(4,128)}), f32[15,4,256]{2,1,0:T(4,128)S(1)}, s32[]{:S(2)}) async-start(f32[16,4,256]{2,1,0:T(4,128)} %copy-done.15), calls=%async_computation.1 | async-start | bytes 122880 | tf_op jit(solution)/shard_map/slice | solution.py:17
  164.5 266.2 %copy-start.17 = (f32[4,256]{1,0:T(4,128)S(1)}, f32[4,256]{1,0:T(4,128)}, u32[]{:S(2)}) copy-start(f32[4,256]{1,0:T(4,128)} %copy-done.16) | copy-start | bytes 12292
  164.5 266.2 %copy-start.31 = (f32[4]{0:T(128)S(1)}, f32[4]{0:T(128)}, u32[]{:S(2)}) copy-start(f32[4]{0:T(128)} %copy-done.30) | copy-start | bytes 52
  289.5 141.4 %copy-start.13 = (bf16[1408,256]{1,0:T(8,128)(2,1)S(1)}, bf16[1408,256]{1,0:T(8,128)(2,1)}, u32[]{:S(2)}) copy-start(bf16[1408,256]{1,0:T(8,128)(2,1)} %param.19) | copy-start | bytes 2162692
  430.9 3.5 copy-start.5
  435.7 1.2 copy-start.9
  435.7 2.2 copy-start.24
  437.0 3.2 copy-start.32
  447.8 5.8 copy-start.33
  453.6 2.3 copy-start.3
  453.6 2.3 copy-start.20
  453.6 2.3 copy-start.27
  455.9 6.9 %copy-start.6 = (f32[1408,256]{1,0:T(8,128)S(1)}, f32[1408,256]{1,0:T(8,128)}, u32[]{:S(2)}) copy-start(f32[1408,256]{1,0:T(8,128)} %fusion.75) | copy-start | bytes 4325380
  455.9 6.9 %copy-start.7 = (f32[88,1408]{0,1:T(8,128)S(1)}, f32[88,1408]{0,1:T(8,128)}, u32[]{:S(2)}) copy-start(f32[88,1408]{0,1:T(8,128)} %fusion.65) | copy-start | bytes 1486852
  587.8 23.2 %collective-permute-start.4 = (f32[88,48]{0,1:T(8,128)S(1)}, f32[88,48]{0,1:T(8,128)S(1)}, u32[]{:S(2)}, u32[]{:S(2)}) collective-permute-start(f32[88,48]{0,1:T(8,128)S(1)} %get-tuple-element.113), channel_id=1, source_target_pairs={{0,2},{1,3},{2,4},{3,5},{4,6},{5,7},{6,8},{7,9},{8,10},{9,11},{10,... | collective-permute-start | bytes 50696
  589.8 23.3 %collective-permute-start.3 = (f32[88,48]{0,1:T(8,128)S(1)}, f32[88,48]{0,1:T(8,128)S(1)}, u32[]{:S(2)}, u32[]{:S(2)}) collective-permute-start(f32[88,48]{0,1:T(8,128)S(1)} %get-tuple-element.113), channel_id=1, source_target_pairs={{0,1},{1,2},{2,3},{3,4},{4,5},{5,6},{6,7},{7,8},{8,9},{9,10},{10,1... | collective-permute-start | bytes 50696
  591.7 16.9 %collective-permute-start.5 = (f32[88,28]{0,1:T(8,128)S(1)}, f32[88,28]{0,1:T(8,128)S(1)}, u32[]{:S(2)}, u32[]{:S(2)}) collective-permute-start(f32[88,28]{0,1:T(8,128)S(1)} %slice.100), channel_id=1, source_target_pairs={{0,3},{1,4},{2,5},{3,6},{4,7},{5,8},{6,9},{7,10},{8,11},{9,12},{10... | collective-permute-start | bytes 29576
  595.6 39.3 %collective-permute-start.1 = (f32[48,264]{1,0:T(8,128)S(1)}, f32[48,264]{1,0:T(8,128)S(1)}, u32[]{:S(2)}, u32[]{:S(2)}) collective-permute-start(f32[48,264]{1,0:T(8,128)S(1)} %get-tuple-element.112), channel_id=1, source_target_pairs={{0,2},{1,3},{2,4},{3,5},{4,6},{5,7},{6,8},{7,9},{8,10},{9,11},{10,... | collective-permute-start | bytes 152072
  606.6 28.3 %collective-permute-start = (f32[48,264]{1,0:T(8,128)S(1)}, f32[48,264]{1,0:T(8,128)S(1)}, u32[]{:S(2)}, u32[]{:S(2)}) collective-permute-start(f32[48,264]{1,0:T(8,128)S(1)} %get-tuple-element.112), channel_id=1, source_target_pairs={{0,1},{1,2},{2,3},{3,4},{4,5},{5,6},{6,7},{7,8},{8,9},{9,10},{10,1... | collective-permute-start | bytes 152072
  608.6 17.5 %collective-permute-start.7 = (f32[48,256]{1,0:T(8,128)S(1)}, f32[48,256]{1,0:T(8,128)S(1)}, u32[]{:S(2)}, u32[]{:S(2)}) collective-permute-start(f32[48,256]{1,0:T(8,128)S(1)} %get-tuple-element.114), channel_id=1, source_target_pairs={{0,2},{1,3},{2,4},{3,5},{4,6},{5,7},{6,8},{7,9},{8,10},{9,11},{10,... | collective-permute-start | bytes 147464
  611.1 15.0 %collective-permute-start.6 = (f32[48,256]{1,0:T(8,128)S(1)}, f32[48,256]{1,0:T(8,128)S(1)}, u32[]{:S(2)}, u32[]{:S(2)}) collective-permute-start(f32[48,256]{1,0:T(8,128)S(1)} %get-tuple-element.114), channel_id=1, source_target_pairs={{0,1},{1,2},{2,3},{3,4},{4,5},{5,6},{6,7},{7,8},{8,9},{9,10},{10,1... | collective-permute-start | bytes 147464
  613.0 11.1 %collective-permute-start.8 = (f32[28,256]{1,0:T(8,128)S(1)}, f32[28,256]{1,0:T(8,128)S(1)}, u32[]{:S(2)}, u32[]{:S(2)}) collective-permute-start(f32[28,256]{1,0:T(8,128)S(1)} %slice.101), channel_id=1, source_target_pairs={{0,3},{1,4},{2,5},{3,6},{4,7},{5,8},{6,9},{7,10},{8,11},{9,12},{10... | collective-permute-start | bytes 86024
  624.1 10.8 %collective-permute-start.2 = (f32[28,264]{1,0:T(8,128)S(1)}, f32[28,264]{1,0:T(8,128)S(1)}, u32[]{:S(2)}, u32[]{:S(2)}) collective-permute-start(f32[28,264]{1,0:T(8,128)S(1)} %slice.99), channel_id=1, source_target_pairs={{0,3},{1,4},{2,5},{3,6},{4,7},{5,8},{6,9},{7,10},{8,11},{9,12},{10... | collective-permute-start | bytes 88712
Sparse Core Ops, SparseCore 0:
  10.1 43.5 all-gather.8
where the time goes:
time: 645 us; the launch traced here: 643 us
  blocking collectives  363 us (56%)
  loops' own time  65.7 us (10%)
  waiting for transfers between devices  55.4 us (9%)
  local copies, waits for them, and re-layouts  54.8 us (8%)
  matrix products  34.9 us (5%)
  starting transfers between devices  27.4 us (4%)
  other arithmetic  24.6 us (4%)
  between operations  16.7 us (3%)
    unnamed x2, blocking collectives  149 us
    psum x1, blocking collectives, local(): t_pooled = lax.psum(t_partial, ('frame', 'crop'))  123 us
    another operation x1, loops' own time, combined_all(): lax.scan(lambda running, share: (join(running, share), None), head, tail)  65.7 us
    all_gather x2, blocking collectives, combined_all(): pieces = jax.tree.map(lambda part: lax.all_gather(part, axis), value)  46.1 us
    psum x1, blocking collectives, local(): s_summed = lax.psum(s_partial, 'frame')  45 us
    all_gather x1, waiting for transfers between devices, local(): gathered = lax.all_gather(tokens, 'frame', axis=0, tiled=True)  39.3 us
    unnamed x9, starting transfers between devices  27.4 us
    dynamic_slice x30, local copies, waits for them, and re-layouts, combined_all(): lax.scan(lambda running, share: (join(running, share), None), head, tail)  18.4 us
  transfers between devices with their start and end apart: 10, of which 3 were waited for; matrix products, arithmetic and copies ran while one was open for 1% of the time, Pallas kernels for 0%

commit v1 on v0

--- a/solution.py
+++ b/solution.py
@@ -113,7 +113,9 @@
         axis=1,
     )
     local_mean = jnp.dot(picks, frame_sums, precision=HIGH) / local_count
-    t_pooled = lax.psum(t_partial, ("frame", "crop"))
+    t_pooled = t_partial
+    for name in ("crop", "frame"):
+        t_pooled = lax.psum(t_pooled, name)
     s_summed = lax.psum(s_partial, "frame")
     s_pooled = local_mean + s_summed
     protos = prototypes.astype(jnp.float32)

time: 645 us -> 520 us (0.81)
  the two profiles are of different devices: /device:TPU:26 before, /device:TPU:18 now
where the time goes in v1:
time: 520 us; the launch traced here: 518 us
  blocking collectives  242 us (47%)
  loops' own time  63.4 us (12%)
  waiting for transfers between devices  56.6 us (11%)
  local copies, waits for them, and re-layouts  52.4 us (10%)
  matrix products  35.4 us (7%)
  starting transfers between devices  30.9 us (6%)
  other arithmetic  21.6 us (4%)
  between operations  16.5 us (3%)
    unnamed x2, blocking collectives  145 us
    another operation x1, loops' own time, combined_all(): lax.scan(lambda running, share: (join(running, share), None), head, tail)  63.4 us
    psum x1, blocking collectives, local(): s_summed = lax.psum(s_partial, 'frame')  47.1 us
    all_gather x1, waiting for transfers between devices, local(): gathered = lax.all_gather(tokens, 'frame', axis=0, tiled=True)  41.3 us
    all_gather x2, blocking collectives, combined_all(): pieces = jax.tree.map(lambda part: lax.all_gather(part, axis), value)  38.8 us
    unnamed x9, starting transfers between devices  30.9 us
    dynamic_slice x30, local copies, waits for them, and re-layouts, combined_all(): lax.scan(lambda running, share: (join(running, share), None), head, tail)  17.8 us
    unnamed x10, waiting for transfers between devices  15.4 us
  transfers between devices with their start and end apart: 10, of which 3 were waited for; matrix products, arithmetic and copies ran while one was open for 2% of the time, Pallas kernels for 0%

profile of v1, /device:TPU:18, one launch (start us, length us, event | category | flops | bytes accessed | tf_op | source)
XLA Modules:
  0.0 518.4 jit_solution(5337795691190359406)
XLA Ops:
  7.2 0.7 all-gather.9.cloned.1.call-update
  7.9 0.8 copy.44
  8.8 1.3 dynamic-slice
  10.8 0.8 convert_reduce_fusion.3
  11.6 1.0 convert_reduce_fusion.2
  12.5 0.7 compare_and_fusion
  13.2 41.3 %all-gather.9.cloned.1.call-done = bf16[16,1,64,1408]{3,2,1,0:T(8,128)(2,1)} async-done(((bf16[1,1,64,1408]{3,2,1,0:T(8,128)(2,1)}), bf16[16,1,64,1408]{3,2,1,0:T(8,128)(2,1)}) %all-gather.9.cloned.1.call-update) | async-done | bytes 2883600 | tf_op jit(solution)/shard_map/all_gather | solution.py:82
  54.5 2.8 convert_reduce_fusion
  57.3 0.9 fusion.16
  58.4 1.8 fusion.26
  60.2 1.9 gather_fusion
  62.2 4.5 reshape.311
  66.7 1.3 copy_select_fusion
  68.5 6.9 %fusion.83 = (f32[256,8]{1,0:T(8,128)S(1)}, f32[256,8,8]{1,2,0:T(8,128)S(1)}) fusion(f32[256,8,8]{1,2,0:T(8,128)S(1)} %convolution_multiply_fusion.2), kind=kOutput, calls=%fused_computation.133 | output fusion | flops 32775 | bytes 139264 | tf_op jit(solution)/shard_map/sub | solution.py:36
  76.4 2.7 fusion.29
  79.1 2.7 convert_element_type.84
  81.9 2.0 fusion.82
  83.9 0.7 convolution_multiply_fusion.3
  84.5 1.0 fusion.38
  85.5 1.4 fusion.39
  86.9 1.2 convolution_reduce_fusion.1
  88.1 10.6 %psum.22 = f32[1408]{0:T(1024)S(1)} all-reduce(f32[1408]{0:T(1024)S(1)} %add_multiply_fusion), channel_id=1, replica_groups=mesh['frame'=16,'crop'=4,'dp'=8] {'crop'}, use_global_device_ids=true, to_apply=%region_16.17 | all-reduce | flops 1408 | bytes 11264 | tf_op jit(solution)/shard_map/psum | solution.py:118
  99.0 47.1 %all-reduce.14 = (f32[4,1408]{1,0:T(4,128)S(1)}, f32[1408]{0:T(1024)S(1)}) all-reduce(f32[4,1408]{1,0:T(4,128)S(1)} %fusion.67, f32[1408]{0:T(1024)S(1)} %psum.22), channel_id=1, replica_groups=mesh['frame'=16,'crop'=4,'dp'=8] {'frame'}, use_global_device_ids=true, to_apply=%region_8.9 | all-reduce | flops 7040 | bytes 56320 | tf_op jit(solution)/shard_map/psum | solution.py:119
  146.2 1.6 multiply_reduce_fusion.1
  147.9 0.7 fusion.84
  148.8 0.9 convolution_bitcast_fusion.5
  149.7 20.8 %all-gather.5 = f32[16,4,256]{2,1,0:T(4,128)S(1)} all-gather(f32[1,4,256]{2,1,0:T(4,128)S(1)} %convolution_bitcast_fusion.5), channel_id=5, replica_groups=mesh['frame'=16,'crop'=4,'dp'=8] {'frame'}, dimensions={0}, use_global_device_ids=true | all-gather | bytes 69632 | tf_op jit(solution)/shard_map/all_gather | solution.py:15
  173.3 1.3 fusion.81
  174.5 0.9 convolution_bitcast_fusion.6
  175.4 18.0 %all-gather.6 = f32[16,1,256]{2,1,0:T(1,128)S(1)} all-gather(f32[1,1,256]{2,1,0:T(1,128)S(1)} %convolution_bitcast_fusion.6), channel_id=6, replica_groups=mesh['frame'=16,'crop'=4,'dp'=8] {'frame'}, dimensions={0}, use_global_device_ids=true | all-gather | bytes 17408 | tf_op jit(solution)/shard_map/all_gather | solution.py:15
  193.9 1.3 dynamic-update-slice.2
  195.3 1.4 dynamic-update-slice.3
  196.7 24.9 %all-reduce.13 = (f32[64]{0:T(128)S(1)}, f32[64]{0:T(128)S(1)}, f32[16]{0:T(128)}, f32[16]{0:T(128)}) all-reduce(f32[64]{0:T(128)S(1)} %dynamic-update-slice, f32[64]{0:T(128)S(1)} %dynamic-update-slice.1, f32[16]{0:T(128)S(1)} %dynamic-update-slice.2, f32[16]{0:T(128)S(1)} %dynamic-update-slice.3), channel_id=3, replica_groups=mesh['frame'=16,'crop'=4,'dp'=8] {'frame'}, use_global_device_ids=true, to_apply=%add.3 | all-reduce | flops 160 | bytes 1280
  221.9 0.7 slice.72
  222.6 0.7 slice.73
  223.3 83.0 %while.20 = (s32[]{:T(128)}, f32[4]{0:T(128)S(1)}, f32[4]{0:T(128)S(1)}, f32[4,256]{1,0:T(4,128)S(1)}, f32[]{:T(128)}, /*index=5*/f32[]{:T(128)}, f32[256]{0:T(2...) while((s32[]{:T(128)}, f32[4]{0:T(128)S(1)}, ...), condition=%wide.region_22.23_spmd, body=%wide.region_21.22_spmd.sunk | while | flops 3872 | bytes 17849 | solution.py:18
  306.3 0.6 broadcast_divide_fusion
  307.2 1.9 fusion.76
  309.5 2.0 fusion.36
  312.0 1.3 convolution_bitcast_fusion.1
  313.2 1.2 convolution_bitcast_fusion.2
  314.5 1.0 convolution_bitcast_fusion.3
  315.4 2.2 fusion.65
  317.6 2.5 fusion.75
  320.4 2.0 copy.54
  322.4 2.8 reshape.240
  325.2 5.8 %copy.55 = bf16[32,64,264]{2,0,1:T(8,128)(2,1)} copy(bf16[32,64,264]{1,0,2:T(8,128)(2,1)S(1)} %reshape.240) | data formatting | bytes 2162688 | tf_op jit(solution)/shard_map/reshape | solution.py:158
  331.0 1.9 fusion.59
  333.3 6.9 %convolution_bitcast_fusion = f32[1408,264]{1,0:T(8,128)} fusion(f32[16,64,264]{2,0,1:T(8,128)S(1)} %fusion.59, bf16[16,1,64,1408]{3,2,1,0:T(8,128)(2,1)S(1)} %copy-done.3, f32[16,64]{1,0:T(8,128)S(1)} %add_rsqrt_fusion, f32[16,64]{1,0:T(8,128)S(1)} %broadcast_multiply_fusion), kind=kOutput, calls=%fused_computation.27 | convolution fusion | flops 4573364224 | bytes 5459968 | tf_op jit(solution)/shard_map/fpd,fpc->dc/dot_general | solution.py:163
  340.2 120.3 %fusion.79 = (f32[48,264]{1,0:T(8,128)S(1)}, f32[88,48]{0,1:T(8,128)S(1)}, f32[48,256]{1,0:T(8,128)S(1)}) fusion(f32[1408,264]{1,0:T(8,128)} %convolution_bitcast_fusion, f32[88,1408]{0,1:T(8,128)S(1)} %copy-done.7, f32[1408,256]{1,0:T(8,128)S(1)} %copy-done.6), kind=kCustom, calls=%all-reduce-scatter.3 | all-reduce-scatter fusion | flops 933889 | bytes 3543040
  460.5 1.9 collective-permute-start.4
  462.4 4.3 collective-permute-start.3
  466.7 1.9 collective-permute-start.5
  468.7 1.3 dynamic-slice.12
  470.6 12.0 %collective-permute-start.1 = (f32[48,264]{1,0:T(8,128)S(1)}, f32[48,264]{1,0:T(8,128)S(1)}, u32[]{:S(2)}, u32[]{:S(2)}) collective-permute-start(f32[48,264]{1,0:T(8,128)S(1)} %get-tuple-element.114), channel_id=1, source_target_pairs={{0,2},{1,3},{2,4},{3,5},{4,6},{5,7},{6,8},{7,9},{8,10},{9,11},{10,... | collective-permute-start | bytes 152072
  482.6 1.9 collective-permute-start
  484.6 2.5 collective-permute-start.7
  487.1 1.9 collective-permute-start.6
  489.0 2.5 collective-permute-start.8
  492.6 7.0 %collective-permute-done.8 = f32[28,256]{1,0:T(8,128)S(1)} collective-permute-done((f32[28,256]{1,0:T(8,128)S(1)}, f32[28,256]{1,0:T(8,128)S(1)}, u32[]{:S(2)}, u32[]{:S(2)}) %collective-permute-start.8) | collective-permute-done | bytes 28704
  499.6 1.9 collective-permute-start.2
  502.0 0.6 constant_dynamic-slice_fusion.3
  502.7 7.7 %collective-permute-done.2 = f32[28,264]{1,0:T(8,128)S(1)} collective-permute-done((f32[28,264]{1,0:T(8,128)S(1)}, f32[28,264]{1,0:T(8,128)S(1)}, u32[]{:S(2)}, u32[]{:S(2)}) %collective-permute-start.2) | collective-permute-done | bytes 29600
  510.9 0.6 constant_dynamic-slice_fusion.5
  (179 shorter events, 28.9 us)
Async XLA Ops:
  7.2 140.7 %copy-start = (bf16[256,2048]{1,0:T(8,128)(2,1)S(1)}, bf16[256,2048]{1,0:T(8,128)(2,1)}, u32[]{:S(2)}) copy-start(bf16[256,2048]{1,0:T(8,128)(2,1)} %param.20) | copy-start | bytes 3145732
  7.2 47.3 %all-gather.9.cloned.1.call-start = ((), (), s32[]{:S(2)}) async-start(), calls=%async_computation | async-start | bytes 3063808 | tf_op jit(solution)/shard_map/all_gather | solution.py:82
  54.5 2.8 copy-start.1
  57.3 1.1 copy-start.13
  68.0 7.5 %copy-start.4 = (bf16[8,256,1,3,88]{4,0,1,3,2:T(8,128)(2,1)}, bf16[8,256,1,3,88]{4,0,1,3,2:T(8,128)(2,1)S(1)}, u32[]{:S(2)}) copy-start(bf16[8,256,1,3,88]{4,0,1,3,2:T(8,128)(2,1)S(1)} %copy_select_fusion) | copy-start | bytes 3244036
  68.5 7.9 %copy-start.2 = (bf16[16,1,64,1408]{3,2,1,0:T(8,128)(2,1)S(1)}, bf16[16,1,64,1408]{3,2,1,0:T(8,128)(2,1)}, u32[]{:S(2)}) copy-start(bf16[16,1,64,1408]{3,2,1,0:T(8,128)(2,1)} %all-gather.9.cloned.1.call-done) | copy-start | bytes 8650756
  68.5 7.9 %copy-start.14 = (bf16[1408,264]{0,1:T(8,128)(2,1)S(1)}, bf16[1408,264]{0,1:T(8,128)(2,1)}, u32[]{:S(2)}) copy-start(bf16[1408,264]{0,1:T(8,128)(2,1)} %param.14) | copy-start | bytes 2230276
  75.5 0.8 copy-start.8
  83.9 14.9 %copy-start.10 = (bf16[88,1408]{1,0:T(8,128)(2,1)S(1)}, bf16[88,1408]{1,0:T(8,128)(2,1)}, u32[]{:S(2)}) copy-start(bf16[88,1408]{1,0:T(8,128)(2,1)} %param.18) | copy-start | bytes 743428
  85.5 85.0 %copy-start.11 = (bf16[1408,256]{1,0:T(8,128)(2,1)S(1)}, bf16[1408,256]{1,0:T(8,128)(2,1)}, u32[]{:S(2)}) copy-start(bf16[1408,256]{1,0:T(8,128)(2,1)} %param.16) | copy-start | bytes 2162692
  147.8 24.8 %copy-start.12 = (f32[2048]{0:T(1024)S(1)}, f32[2048]{0:T(1024)}, u32[]{:S(2)}) copy-start(f32[2048]{0:T(1024)} %param.21) | copy-start | bytes 24580
  307.2 4.8 copy-start.5
  313.2 1.2 copy-start.9
  331.0 2.3 copy-start.3
  333.3 6.9 %copy-start.6 = (f32[1408,256]{1,0:T(8,128)S(1)}, f32[1408,256]{1,0:T(8,128)}, u32[]{:S(2)}) copy-start(f32[1408,256]{1,0:T(8,128)} %fusion.75) | copy-start | bytes 4325380
  333.3 6.9 %copy-start.7 = (f32[88,1408]{0,1:T(8,128)S(1)}, f32[88,1408]{0,1:T(8,128)}, u32[]{:S(2)}) copy-start(f32[88,1408]{0,1:T(8,128)} %fusion.65) | copy-start | bytes 1486852
  460.5 26.6 %collective-permute-start.4 = (f32[88,48]{0,1:T(8,128)S(1)}, f32[88,48]{0,1:T(8,128)S(1)}, u32[]{:S(2)}, u32[]{:S(2)}) collective-permute-start(f32[88,48]{0,1:T(8,128)S(1)} %get-tuple-element.115), channel_id=1, source_target_pairs={{0,2},{1,3},{2,4},{3,5},{4,6},{5,7},{6,8},{7,9},{8,10},{9,11},{10,... | collective-permute-start | bytes 50696
  462.4 26.6 %collective-permute-start.3 = (f32[88,48]{0,1:T(8,128)S(1)}, f32[88,48]{0,1:T(8,128)S(1)}, u32[]{:S(2)}, u32[]{:S(2)}) collective-permute-start(f32[88,48]{0,1:T(8,128)S(1)} %get-tuple-element.115), channel_id=1, source_target_pairs={{0,1},{1,2},{2,3},{3,4},{4,5},{5,6},{6,7},{7,8},{8,9},{9,10},{10,1... | collective-permute-start | bytes 50696
  466.7 17.8 %collective-permute-start.5 = (f32[88,28]{0,1:T(8,128)S(1)}, f32[88,28]{0,1:T(8,128)S(1)}, u32[]{:S(2)}, u32[]{:S(2)}) collective-permute-start(f32[88,28]{0,1:T(8,128)S(1)} %slice.100), channel_id=1, source_target_pairs={{0,3},{1,4},{2,5},{3,6},{4,7},{5,8},{6,9},{7,10},{8,11},{9,12},{10... | collective-permute-start | bytes 29576
  470.6 39.8 %collective-permute-start.1 = (f32[48,264]{1,0:T(8,128)S(1)}, f32[48,264]{1,0:T(8,128)S(1)}, u32[]{:S(2)}, u32[]{:S(2)}) collective-permute-start(f32[48,264]{1,0:T(8,128)S(1)} %get-tuple-element.114), channel_id=1, source_target_pairs={{0,2},{1,3},{2,4},{3,5},{4,6},{5,7},{6,8},{7,9},{8,10},{9,11},{10,... | collective-permute-start | bytes 152072
  482.6 27.8 %collective-permute-start = (f32[48,264]{1,0:T(8,128)S(1)}, f32[48,264]{1,0:T(8,128)S(1)}, u32[]{:S(2)}, u32[]{:S(2)}) collective-permute-start(f32[48,264]{1,0:T(8,128)S(1)} %get-tuple-element.114), channel_id=1, source_target_pairs={{0,1},{1,2},{2,3},{3,4},{4,5},{5,6},{6,7},{7,8},{8,9},{9,10},{10,1... | collective-permute-start | bytes 152072
  484.6 17.0 %collective-permute-start.7 = (f32[48,256]{1,0:T(8,128)S(1)}, f32[48,256]{1,0:T(8,128)S(1)}, u32[]{:S(2)}, u32[]{:S(2)}) collective-permute-start(f32[48,256]{1,0:T(8,128)S(1)} %get-tuple-element.116), channel_id=1, source_target_pairs={{0,2},{1,3},{2,4},{3,5},{4,6},{5,7},{6,8},{7,9},{8,10},{9,11},{10,... | collective-permute-start | bytes 147464
  487.1 14.5 %collective-permute-start.6 = (f32[48,256]{1,0:T(8,128)S(1)}, f32[48,256]{1,0:T(8,128)S(1)}, u32[]{:S(2)}, u32[]{:S(2)}) collective-permute-start(f32[48,256]{1,0:T(8,128)S(1)} %get-tuple-element.116), channel_id=1, source_target_pairs={{0,1},{1,2},{2,3},{3,4},{4,5},{5,6},{6,7},{7,8},{8,9},{9,10},{10,1... | collective-permute-start | bytes 147464
  489.0 10.6 %collective-permute-start.8 = (f32[28,256]{1,0:T(8,128)S(1)}, f32[28,256]{1,0:T(8,128)S(1)}, u32[]{:S(2)}, u32[]{:S(2)}) collective-permute-start(f32[28,256]{1,0:T(8,128)S(1)} %slice.101), channel_id=1, source_target_pairs={{0,3},{1,4},{2,5},{3,6},{4,7},{5,8},{6,9},{7,10},{8,11},{9,12},{10... | collective-permute-start | bytes 86024
  499.6 10.8 %collective-permute-start.2 = (f32[28,264]{1,0:T(8,128)S(1)}, f32[28,264]{1,0:T(8,128)S(1)}, u32[]{:S(2)}, u32[]{:S(2)}) collective-permute-start(f32[28,264]{1,0:T(8,128)S(1)} %slice.99), channel_id=1, source_target_pairs={{0,3},{1,4},{2,5},{3,6},{4,7},{5,8},{6,9},{7,10},{8,11},{9,12},{10... | collective-permute-start | bytes 88712
Sparse Core Ops, SparseCore 0:
  10.1 44.3 all-gather.8
